TPU v7x, 32 devices: a whole 2x2x4 slice. The times are simulated.
32 devices in a mesh: sec: 4 (over y, x), strip: 8 (over z, core).
Axes of the slice: x: 2, y: 2, z: 4, core: 2. Of those that a mesh axis runs over, the one named last changes fastest.
Arguments:
- features: bfloat16 [4, 96, 128, 128], P('sec', 'strip'), may hold values from -6 to 6
- offsets: int32 [4], replicated, may hold values from -2 to 2
- state: float32 [2, 4, 96, 128], P(None, 'sec', 'strip'), may hold values from -6 to 6
- w_first: bfloat16 [3, 3, 162, 128], replicated, may hold values from -0.15625 to 0.15625
- b_first: float32 [128], replicated, may hold values from -3 to 3
- w_second: bfloat16 [3, 3, 128, 128], replicated, may hold values from -0.1875 to 0.1875
- b_second: float32 [128], replicated, may hold values from -3 to 3
- w_third: bfloat16 [3, 3, 128, 2], replicated, may hold values from -0.1875 to 0.1875
Outputs:
- updated: float32 [2, 4, 96, 128], P(None, 'sec', 'strip')
Inputs may be any that keep to these rules, and one draw needn't show every extreme that they name: offsets[s] is the integer row offset of section s+1 against section s; the last entry is not used.
All inputs are finite; a program needn't handle non-finite values.
Results may differ from a plain program's by a relative error of at most 0.0029.
Values may be sent and summed in bfloat16 or wider, within the bound.
A program may use at most 64 MiB of HBM per device.

v0:
```python
import jax
import jax.numpy as jnp
from jax import lax
from jax.sharding import PartitionSpec as P

C = 128


def passed_along(x, axis, by):
    length = lax.axis_size(axis)
    pairs = [(i, i + by) for i in range(length) if 0 <= i + by < length]
    return lax.ppermute(x, axis, pairs)


def extended(cells, sides, width):
    for axis, dim in sides:
        count = lax.axis_size(axis)
        ends = count - 1
        head = lax.slice_in_dim(cells, 0, width, axis=dim)
        tail = lax.slice_in_dim(cells, cells.shape[dim] - width, cells.shape[dim], axis=dim)
        cells = jnp.concatenate(
            [
                lax.ppermute(tail, axis, [(i, (i + 1) % count) for i in range(ends)]),
                cells,
                lax.ppermute(head, axis, [((i + 1) % count, i) for i in range(ends)]),
            ],
            axis=dim,
        )
    return cells


def band_corr(mine, other, shift, extra):
    rows, cols, chans = mine.shape
    padded = jnp.pad(other, ((0, 0), (4, 4), (0, 0)))
    reach = jnp.arange(cols + 8)[:, None] - jnp.arange(cols)[None, :]
    select = (reach[None] == jnp.arange(9)[:, None, None]).astype(jnp.float32)
    planes = []
    for row_step in range(-4, 5):
        start = extra + row_step + shift
        taken = lax.dynamic_slice_in_dim(padded, start, rows, 0)
        products = jnp.einsum("rjc,ric->rji", taken, mine, preferred_element_type=jnp.float32)
        band = jnp.sum(products[None] * select[:, None], axis=2)
        planes.append(band)
    return jnp.concatenate(planes, 0)


def convolve(values, kernel, layout, rows_pad):
    return lax.conv_general_dilated(
        values[None],
        kernel,
        (1, 1),
        ((rows_pad, rows_pad), (1, 1)),
        dimension_numbers=(layout, "HWIO", "NHWC"),
        preferred_element_type=jnp.float32,
    )[0]


def clip_rows(values, lead):
    count = values.shape[0]
    rows_dev = count - 2 * lead
    global_row = lax.axis_index("strip") * rows_dev + jnp.arange(count) - lead
    inside = (global_row >= 0) & (global_row < rows_dev * lax.axis_size("strip"))
    return jnp.where(inside[:, None, None], values, 0.0)


def body(features, offsets, state, w_first, b_first, w_second, b_second, w_third):
    mine = features[0]
    sec_index = lax.axis_index("sec")
    above = passed_along(features, "sec", -1)[0]
    below = passed_along(features, "sec", 1)[0]
    shift_above = offsets[sec_index]
    shift_below = jnp.where(sec_index > 0, -offsets[jnp.maximum(sec_index - 1, 0)], 0)
    neighbours = jnp.stack([below, above])
    scale = C ** (-0.5)
    mine_wide = extended(mine, (("strip", 0),), 3)
    wide = extended(neighbours, (("strip", 1),), 9)
    corr = jnp.concatenate(
        [
            band_corr(mine_wide, wide[0], shift_below, 6),
            band_corr(mine_wide, wide[1], shift_above, 6),
        ],
        0,
    )
    corr = (corr * scale).astype(jnp.bfloat16)
    hidden_one = jax.nn.relu(convolve(corr, w_first, "NCHW", 0) + b_first)
    hidden_one = clip_rows(hidden_one, 2).astype(jnp.bfloat16)
    hidden_two = jax.nn.relu(convolve(hidden_one, w_second, "NHWC", 0) + b_second)
    hidden_two = clip_rows(hidden_two, 1).astype(jnp.bfloat16)
    delta = convolve(hidden_two, w_third, "NHWC", 0)
    return state + jnp.moveaxis(delta, 2, 0)[:, None]


def solution(mesh):
    in_specs = (
        P("sec", "strip", None, None),
        P(),
        P(None, "sec", "strip", None),
        P(),
        P(),
        P(),
        P(),
        P(),
    )
    out_specs = P(None, "sec", "strip", None)
    return jax.shard_map(body, mesh=mesh, in_specs=in_specs, out_specs=out_specs, check_vma=False)
```

profile of v0, /device:TPU:18, one launch (start us, length us, event | category | flops | bytes accessed | tf_op | source)
XLA Modules:
  0.0 109.7 jit_solution(11181904368599783615)
XLA Ops:
  0.0 3.5 %collective-permute-start = (bf16[1,12,128,128]{3,2,1,0:T(8,128)(2,1)}, bf16[1,12,128,128]{3,2,1,0:T(8,128)(2,1)S(1)}, u32[]{:S(2)}, u32[]{:S(2)}) collective-permute-start(bf16[1,12,128,128]{3,2,1,0:T(8,128)(2,1)} %param.8), channel_id=1, source_target_pairs={{0,8},{8,16},{16,24},{1,9},{9,17},{17,25},{2,10},{10,18},{18,26},{... | collective-permute-start | bytes 1179656 | tf_op jit(solution)/shard_map/ppermute | solution.py:12
  3.5 2.5 %collective-permute-start.1 = (bf16[1,12,128,128]{3,2,1,0:T(8,128)(2,1)}, bf16[1,12,128,128]{3,2,1,0:T(8,128)(2,1)S(1)}, u32[]{:S(2)}, u32[]{:S(2)}) collective-permute-start(bf16[1,12,128,128]{3,2,1,0:T(8,128)(2,1)} %param.8), channel_id=1, source_target_pairs={{8,0},{16,8},{24,16},{9,1},{17,9},{25,17},{10,2},{18,10},{26,18},{... | collective-permute-start | bytes 1179656 | tf_op jit(solution)/shard_map/ppermute | solution.py:12
  6.0 7.3 %collective-permute-done = bf16[1,12,128,128]{3,2,1,0:T(8,128)(2,1)S(1)} collective-permute-done((bf16[1,12,128,128]{3,2,1,0:T(8,128)(2,1)}, bf16[1,12,128,128]{3,2,1,0:T(8,128)(2,1)S(1)}, u32[]{:S(2)}, u32[]{:S(2)}) %collective-permute-start) | collective-permute-done | bytes 393248 | tf_op jit(solution)/shard_map/ppermute | solution.py:12
  13.4 9.1 %collective-permute-done.1 = bf16[1,12,128,128]{3,2,1,0:T(8,128)(2,1)S(1)} collective-permute-done((bf16[1,12,128,128]{3,2,1,0:T(8,128)(2,1)}, bf16[1,12,128,128]{3,2,1,0:T(8,128)(2,1)S(1)}, u32[]{:S(2)}, u32[]{:S(2)}) %collective-permute-start.1) | collective-permute-done | bytes 393248 | tf_op jit(solution)/shard_map/ppermute | solution.py:12
  22.5 0.1 constant_dynamic-update-slice_fusion
  22.5 1.0 fusion.160
  23.5 1.9 %collective-permute-start.2 = (bf16[2,9,128,128]{3,2,1,0:T(8,128)(2,1)}, bf16[2,9,128,128]{3,2,1,0:T(8,128)(2,1)S(1)}, u32[]{:S(2)}, u32[]{:S(2)}) collective-permute-start(bf16[2,9,128,128]{3,2,1,0:T(8,128)(2,1)} %get-tuple-element.25), channel_id=1, source_target_pairs={{0,1},{1,2},{2,3},{3,4},{4,5},{5,6},{6,7},{8,9},{9,10},{10,11},{11... | collective-permute-start | bytes 1769480 | tf_op jit(solution)/shard_map/ppermute | solution.py:23
  25.4 3.6 %collective-permute-start.3 = (bf16[2,9,128,128]{3,2,1,0:T(8,128)(2,1)S(1)}, bf16[2,9,128,128]{3,2,1,0:T(8,128)(2,1)S(1)}, u32[]{:S(2)}, u32[]{:S(2)}) collective-permute-start(bf16[2,9,128,128]{3,2,1,0:T(8,128)(2,1)S(1)} %get-tuple-element.26), channel_id=1, source_target_pairs={{1,0},{2,1},{3,2},{4,3},{5,4},{6,5},{7,6},{9,8},{10,9},{11,10},{12... | collective-permute-start | bytes 1769480 | tf_op jit(solution)/shard_map/ppermute | solution.py:25
  29.1 0.7 slice_bitcast_fusion.3
  29.8 1.9 %collective-permute-start.4 = (bf16[3,128,128]{2,1,0:T(8,128)(2,1)}, bf16[3,128,128]{2,1,0:T(8,128)(2,1)S(1)}, u32[]{:S(2)}, u32[]{:S(2)}) collective-permute-start(bf16[3,128,128]{2,1,0:T(8,128)(2,1)} %get-tuple-element.31), channel_id=1, source_target_pairs={{0,1},{1,2},{2,3},{3,4},{4,5},{5,6},{6,7},{8,9},{9,10},{10,11},{11... | collective-permute-start | bytes 294920 | tf_op jit(solution)/shard_map/ppermute | solution.py:23
  31.7 3.6 %collective-permute-start.5 = (bf16[3,128,128]{2,1,0:T(8,128)(2,1)}, bf16[3,128,128]{2,1,0:T(8,128)(2,1)S(1)}, u32[]{:S(2)}, u32[]{:S(2)}) collective-permute-start(bf16[3,128,128]{2,1,0:T(8,128)(2,1)} %get-tuple-element.32), channel_id=1, source_target_pairs={{1,0},{2,1},{3,2},{4,3},{5,4},{6,5},{7,6},{9,8},{10,9},{11,10},{12... | collective-permute-start | bytes 294920 | tf_op jit(solution)/shard_map/ppermute | solution.py:25
  35.4 0.7 fusion.163
  48.2 0.2 pad_maximum_fusion
  48.5 0.1 slice_bitcast_fusion.1
  48.6 0.5 fusion.58
  49.1 0.5 fusion.60
  49.6 0.5 fusion.62
  50.2 0.5 fusion.64
  50.7 0.5 fusion.66
  51.2 0.5 fusion.68
  51.7 0.5 fusion.70
  52.2 0.5 fusion.72
  52.7 0.5 fusion.74
  53.2 0.5 fusion.42
  53.8 0.5 fusion.44
  54.3 0.5 fusion.46
  54.8 0.5 fusion.48
  55.3 0.5 fusion.50
  55.8 0.5 fusion.52
  56.3 0.5 fusion.54
  56.8 0.5 fusion.56
  57.4 0.5 fusion.40
  57.9 33.1 %multiply_reduce_fusion = (f32[9,18,128]{2,1,0:T(8,128)S(1)}, f32[9,18,128]{2,1,0:T(8,128)S(1)}, f32[9,18,128]{2,1,0:T(8,128)S(1)}, f32[9,18,128]{2,1,0:T(8,128)...) fusion(f32[18,136,128]{2,1,0:T(8,128)S(1)} %fusion.40, ...), kind=kLoop, calls=%fused_computation | loop fusion | flops 101150208 | bytes 24680448 | tf_op jit(solution)/shard_map/reduce_sum | solution.py:42
  91.3 0.2 fusion.38
  91.5 1.3 %copy.20 = bf16[162,18,1,128]{0,3,1,2:T(8,128)(2,1)S(1)} copy(bf16[162,18,1,128]{3,1,0,2:T(8,128)(2,1)S(1)} %fusion.38) | data formatting | bytes 1492992
  92.8 0.6 pad.9.clone
  93.4 0.8 reshape.333
  94.1 0.0 copy-start.6
  94.1 0.0 copy-start.8
  94.1 0.3 copy.16
  94.5 0.3 copy-done.6
  94.8 0.0 copy-done.8
  94.8 3.2 %fusion.33 = bf16[16,1,8,17,128]{4,2,3,0,1:T(8,128)(2,1)S(1)} fusion(bf16[3,3,162,128]{3,2,1,0:T(8,128)(2,1)S(1)} %copy-done, bf16[162,18,1,7,2]{0,3,4,1,2:T(8,128)(2,1)S(1)} %slice.42, bf16[162,18,1,8,17]{0,3,4,1,2:T(8,128)(2,1)S(1)} %copy.16, f32[128]{0:T(128)S(1)} %copy-done.6, pred[16]{0:T(512)(128)(4,1)S(1)} %compare_and_fusion, ...), kind=kOutput, calls=%fused_computation.44 | convolution fusion | flops 816518208 | bytes 1805768 | tf_op jit(solution)/shard_map/conv_general_dilated | solution.py:48
  98.1 1.3 %fusion.29 = bf16[14,1,8,17,128]{4,2,3,0,1:T(8,128)(2,1)S(1)} fusion(bf16[3,3,128,128]{3,2,1,0:T(8,128)(2,1)S(1)} %copy-done.4, bf16[16,1,7,1,128]{4,2,3,0,1:T(8,128)(2,1)S(1)} %get-tuple-element.28, bf16[16,1,7,1,128]{4,2,3,0,1:T(8,128)(2,1)S(1)} %get-tuple-element.27, bf16[16,1,8,17,128]{4,2,3,0,1:T(8,128)(2,1)S(1)} %fusion.33, f32[128]{0:T(128)S(1)} %copy-done.7, ...), kind=kOutput, calls=%fused_computation.42 | convolution fusion | flops 565843968 | bytes 1397398 | tf_op jit(solution)/shard_map/conv_general_dilated | solution.py:48
  99.5 9.3 %fusion.90 = f32[12,8,17,2]{1,3,2,0:T(2,128)S(1)} fusion(bf16[3,3,128,2]{2,3,1,0:T(2,128)(2,1)S(1)} %copy-done.5, bf16[14,1,7,1,128]{4,2,3,0,1:T(8,128)(2,1)S(1)} %get-tuple-element.30, bf16[14,1,7,1,128]{4,2,3,0,1:T(8,128)(2,1)S(1)} %get-tuple-element.29, bf16[14,1,8,17,128]{4,2,3,0,1:T(8,128)(2,1)S(1)} %fusion.29), kind=kOutput, calls=%fused_computation.103 | convolution fusion | flops 10244096 | bytes 555264 | tf_op jit(solution)/shard_map/conv_general_dilated | solution.py:48
  108.7 0.2 copy.17
  109.0 0.1 reshape.343
  109.1 0.6 copy.19
  (45 shorter events, 0.4 us)
Async XLA Ops:
  0.0 94.5 %copy-start = (bf16[3,3,162,128]{3,2,1,0:T(8,128)(2,1)S(1)}, bf16[3,3,162,128]{3,2,1,0:T(8,128)(2,1)}, u32[]{:S(2)}) copy-start(bf16[3,3,162,128]{3,2,1,0:T(8,128)(2,1)} %param.11) | copy-start | bytes 1119748
  0.0 29.1 %copy-start.1 = (bf16[1,12,128,128]{3,2,1,0:T(8,128)(2,1)S(1)}, bf16[1,12,128,128]{3,2,1,0:T(8,128)(2,1)}, u32[]{:S(2)}) copy-start(bf16[1,12,128,128]{3,2,1,0:T(8,128)(2,1)} %param.8) | copy-start | bytes 1179652
  0.0 35.3 %copy-start.3 = (s32[4]{0:T(128)S(1)}, s32[4]{0:T(128)}, u32[]{:S(2)}) copy-start(s32[4]{0:T(128)} %param.9) | copy-start | bytes 52
  0.0 13.3 %collective-permute-start = (bf16[1,12,128,128]{3,2,1,0:T(8,128)(2,1)}, bf16[1,12,128,128]{3,2,1,0:T(8,128)(2,1)S(1)}, u32[]{:S(2)}, u32[]{:S(2)}) collective-permute-start(bf16[1,12,128,128]{3,2,1,0:T(8,128)(2,1)} %param.8), channel_id=1, source_target_pairs={{0,8},{8,16},{16,24},{1,9},{9,17},{17,25},{2,10},{10,18},{18,26},{... | collective-permute-start | bytes 1179656 | tf_op jit(solution)/shard_map/ppermute | solution.py:12
  3.5 18.9 %collective-permute-start.1 = (bf16[1,12,128,128]{3,2,1,0:T(8,128)(2,1)}, bf16[1,12,128,128]{3,2,1,0:T(8,128)(2,1)S(1)}, u32[]{:S(2)}, u32[]{:S(2)}) collective-permute-start(bf16[1,12,128,128]{3,2,1,0:T(8,128)(2,1)} %param.8), channel_id=1, source_target_pairs={{8,0},{16,8},{24,16},{9,1},{17,9},{25,17},{10,2},{18,10},{26,18},{... | collective-permute-start | bytes 1179656 | tf_op jit(solution)/shard_map/ppermute | solution.py:12
  23.5 24.7 %collective-permute-start.2 = (bf16[2,9,128,128]{3,2,1,0:T(8,128)(2,1)}, bf16[2,9,128,128]{3,2,1,0:T(8,128)(2,1)S(1)}, u32[]{:S(2)}, u32[]{:S(2)}) collective-permute-start(bf16[2,9,128,128]{3,2,1,0:T(8,128)(2,1)} %get-tuple-element.25), channel_id=1, source_target_pairs={{0,1},{1,2},{2,3},{3,4},{4,5},{5,6},{6,7},{8,9},{9,10},{10,11},{11... | collective-permute-start | bytes 1769480 | tf_op jit(solution)/shard_map/ppermute | solution.py:23
  25.4 22.8 %collective-permute-start.3 = (bf16[2,9,128,128]{3,2,1,0:T(8,128)(2,1)S(1)}, bf16[2,9,128,128]{3,2,1,0:T(8,128)(2,1)S(1)}, u32[]{:S(2)}, u32[]{:S(2)}) collective-permute-start(bf16[2,9,128,128]{3,2,1,0:T(8,128)(2,1)S(1)} %get-tuple-element.26), channel_id=1, source_target_pairs={{1,0},{2,1},{3,2},{4,3},{5,4},{6,5},{7,6},{9,8},{10,9},{11,10},{12... | collective-permute-start | bytes 1769480 | tf_op jit(solution)/shard_map/ppermute | solution.py:25
  29.8 18.8 %collective-permute-start.4 = (bf16[3,128,128]{2,1,0:T(8,128)(2,1)}, bf16[3,128,128]{2,1,0:T(8,128)(2,1)S(1)}, u32[]{:S(2)}, u32[]{:S(2)}) collective-permute-start(bf16[3,128,128]{2,1,0:T(8,128)(2,1)} %get-tuple-element.31), channel_id=1, source_target_pairs={{0,1},{1,2},{2,3},{3,4},{4,5},{5,6},{6,7},{8,9},{9,10},{10,11},{11... | collective-permute-start | bytes 294920 | tf_op jit(solution)/shard_map/ppermute | solution.py:23
  31.7 16.9 %collective-permute-start.5 = (bf16[3,128,128]{2,1,0:T(8,128)(2,1)}, bf16[3,128,128]{2,1,0:T(8,128)(2,1)S(1)}, u32[]{:S(2)}, u32[]{:S(2)}) collective-permute-start(bf16[3,128,128]{2,1,0:T(8,128)(2,1)} %get-tuple-element.32), channel_id=1, source_target_pairs={{1,0},{2,1},{3,2},{4,3},{5,4},{6,5},{7,6},{9,8},{10,9},{11,10},{12... | collective-permute-start | bytes 294920 | tf_op jit(solution)/shard_map/ppermute | solution.py:25
  94.1 0.7 copy-start.6
  94.1 0.7 copy-start.8
  94.8 3.2 %copy-start.4 = (bf16[3,3,128,128]{3,2,1,0:T(8,128)(2,1)S(1)}, bf16[3,3,128,128]{3,2,1,0:T(8,128)(2,1)}, u32[]{:S(2)}) copy-start(bf16[3,3,128,128]{3,2,1,0:T(8,128)(2,1)} %param.13) | copy-start | bytes 884740
  94.8 3.3 %copy-start.7 = (f32[128]{0:T(128)S(1)}, f32[128]{0:T(128)}, u32[]{:S(2)}) copy-start(f32[128]{0:T(128)} %param.14) | copy-start | bytes 1540
  98.1 1.4 %copy-start.5 = (bf16[3,3,128,2]{2,3,1,0:T(2,128)(2,1)S(1)}, bf16[3,3,128,2]{2,3,1,0:T(2,128)(2,1)}, u32[]{:S(2)}) copy-start(bf16[3,3,128,2]{2,3,1,0:T(2,128)(2,1)} %param.15) | copy-start | bytes 13828
  99.5 9.6 %copy-start.2 = (f32[2,1,12,128]{3,1,2,0:T(1,128)S(1)}, f32[2,1,12,128]{3,1,2,0:T(1,128)}, u32[]{:S(2)}) copy-start(f32[2,1,12,128]{3,1,2,0:T(1,128)} %param.10) | copy-start | bytes 36868
where the time goes:
time: 111 us; the launch traced here: 110 us
  other arithmetic  33.6 us (30%)
  matrix products  22.9 us (21%)
  starting transfers between devices  17.1 us (15%)
  waiting for transfers between devices  16.4 us (15%)
  between operations  12.7 us (11%)
  local copies, waits for them, and re-layouts  6.96 us (6%)
    reduce_sum x1, other arithmetic, band_corr(): band = jnp.sum(products[None] * select[:, None], axis=2)  33.1 us
    ppermute x2, waiting for transfers between devices, passed_along(): return lax.ppermute(x, axis, pairs)  16.4 us
    conv_general_dilated x3, matrix products, convolve(): lax.conv_general_dilated(values[None], kernel, (1, 1), ((rows_pad, rows_p...  13.8 us
    dot_general x18, matrix products, band_corr(): jnp.einsum('rjc,ric->rji', taken, mine, preferred_element_type=jnp.float32)  9.1 us
    ppermute x2, starting transfers between devices, extended(): lax.ppermute(head, axis, [((i + 1) % count, i) for i in range(ends)])  7.28 us
    ppermute x2, starting transfers between devices, passed_along(): return lax.ppermute(x, axis, pairs)  5.99 us
    ppermute x2, starting transfers between devices, extended(): lax.ppermute(tail, axis, [(i, (i + 1) % count) for i in range(ends)])  3.82 us
  transfers between devices with their start and end apart: 6, of which 2 were waited for; matrix products, arithmetic and copies ran while one was open for 2% of the time, Pallas kernels for 0%

commit v1 on v0

v1 whole, which is shorter than its diff:
```python
import functools

import jax
import jax.numpy as jnp
from jax import lax
from jax.experimental import pallas as pl
from jax.experimental.pallas import tpu as pltpu
from jax.sharding import PartitionSpec as P

SIDE = 9
STEP = 3
TAPS = 9
VMEM = pl.BlockSpec(memory_space=pltpu.VMEM)
SMEM = pl.BlockSpec(memory_space=pltpu.SMEM)


def group_of(rows):
    return max(g for g in range(1, 8) if rows % g == 0)


def exchange(secs, strips, feat, mine, wide, send_sem, recv_sem):
    rows = feat.shape[1]
    count = rows // STEP
    sec, strip = lax.axis_index("sec"), lax.axis_index("strip")
    odd = lax.rem(sec, 2)
    partner = sec + 1 - 2 * odd
    near, far = 1 - odd, odd
    relay_to, relay_from = sec + 2 - 4 * odd, sec - 2 + 4 * odd
    has_to = (relay_to >= 0) & (relay_to < secs)
    has_from = (relay_from >= 0) & (relay_from < secs)
    has_low, has_high = strip > 0, strip < strips - 1

    barrier = pltpu.get_barrier_semaphore()
    greeted = (
        (None, partner, strip),
        (has_to, relay_to, strip),
        (has_from, relay_from, strip),
        (has_low, sec, strip - 1),
        (has_high, sec, strip + 1),
    )

    def when(cond, act):
        if cond is None:
            act()
        else:
            pl.when(cond)(act)

    for cond, a, b in greeted:
        when(cond, lambda a=a, b=b: pl.semaphore_signal(barrier, inc=1, device_id=(a, b), device_id_type=pl.DeviceIdType.MESH))

    zero = jnp.zeros((SIDE,) + wide.shape[2:], wide.dtype)

    @pl.when(jnp.logical_not(has_from))
    def _():
        wide[far] = jnp.zeros(wide.shape[1:], wide.dtype)

    @pl.when(jnp.logical_not(has_low))
    def _():
        wide[near, 0:SIDE] = zero
        wide[far, 0:SIDE] = zero
        mine[0:STEP] = zero[:STEP]

    @pl.when(jnp.logical_not(has_high))
    def _():
        wide[near, SIDE + rows:] = zero
        wide[far, SIDE + rows:] = zero
        mine[STEP + rows:] = zero[:STEP]

    mine[STEP:STEP + rows] = feat[0]

    pl.semaphore_wait(barrier, 1 + sum(cond.astype(jnp.int32) for cond, _, _ in greeted[1:]))

    waits = []
    number = [0]

    def copy(src, dst, a, b, sends, gets):
        at = number[0]
        number[0] += 1
        made = pltpu.make_async_remote_copy(
            src_ref=src, dst_ref=dst, send_sem=send_sem.at[at], recv_sem=recv_sem.at[at],
            device_id=(a, b), device_id_type=pl.DeviceIdType.MESH,
        )
        when(sends, made.start)
        waits.append((sends, made.wait_send))
        return lambda: when(gets, made.wait_recv)

    def both(x, y):
        return y if x is None else x & y

    def down(slot, q, known):
        return copy(
            wide.at[slot, pl.ds(SIDE + STEP * q, STEP)], wide.at[slot, pl.ds(SIDE + rows + STEP * q, STEP)],
            sec, strip - 1, both(known, has_low), both(known, has_high),
        )

    def up(slot, q, known):
        return copy(
            wide.at[slot, pl.ds(SIDE + STEP * q, STEP)], wide.at[slot, pl.ds(SIDE + STEP * q - rows, STEP)],
            sec, strip + 1, both(known, has_high), both(known, has_low),
        )

    order = list(range(count))
    direct = [
        copy(feat.at[0, pl.ds(STEP * q, STEP)], wide.at[far, pl.ds(SIDE + STEP * q, STEP)], partner, strip, None, None)
        for q in order
    ]
    last = []
    last.append(copy(feat.at[0, pl.ds(0, STEP)], mine.at[pl.ds(STEP + rows, STEP)], sec, strip - 1, has_low, has_high))
    last.append(copy(feat.at[0, pl.ds(rows - STEP, STEP)], mine.at[pl.ds(0, STEP)], sec, strip + 1, has_high, has_low))

    def sides(slot, q, known):
        if STEP * q < SIDE:
            last.append(down(slot, q, known))
        if STEP * q >= rows - SIDE:
            last.append(up(slot, q, known))

    relayed = []
    for q in order + [count]:
        if q < count:
            direct[q]()
            relayed.append(copy(
                wide.at[near, pl.ds(SIDE + STEP * q, STEP)], wide.at[far, pl.ds(SIDE + STEP * q, STEP)],
                relay_to, strip, has_to, has_from,
            ))
            sides(near, q, None)
        if q >= 1:
            relayed[q - 1]()
            sides(far, q - 1, has_from)
    for wait in last:
        wait()
    for cond, wait in waits:
        when(cond, wait)


def convolve(source, weight, bias, target):
    rows, cols, width = target.shape
    depth = source.shape[2]
    group = group_of(rows)
    at_col = lax.broadcasted_iota(jnp.int32, (cols, width), 0)

    def step(g, carry):
        base = g * group
        taken = jnp.concatenate(
            [source[pl.ds(base + d, group)].reshape(group * cols, depth) for d in range(3)], axis=1
        )
        sums = jnp.dot(taken, weight[...], preferred_element_type=jnp.float32)
        for i in range(group):
            one = sums[i * cols:(i + 1) * cols]
            before = jnp.where(at_col == 0, 0.0, pltpu.roll(one[:, :width], 1, 0))
            after = jnp.where(at_col == cols - 1, 0.0, pltpu.roll(one[:, 2 * width:], cols - 1, 0))
            total = one[:, width:2 * width] + before + after + bias[...]
            target[base + i] = jnp.maximum(total, 0.0).astype(target.dtype)
        return carry

    lax.fori_loop(0, rows // group, step, 0)


def skewed(block, shift):
    rows, cols = block.shape
    pieces = []
    start = 0
    for top in range(0, rows, 8):
        if (shift + top) % cols + 7 > cols:
            if top > start:
                pieces.append(pltpu.roll(block[start:top], (shift + start) % cols, 1, stride=1, stride_axis=0))
            crossing = pltpu.roll(block[top:top + 8], (shift + top - 8) % cols, 1, stride=1, stride_axis=0)
            pieces.append(pltpu.roll(crossing, 8, 1))
            start = top + 8
    if start < rows:
        pieces.append(pltpu.roll(block[start:], (shift + start) % cols, 1, stride=1, stride_axis=0))
    return jnp.concatenate(pieces, axis=0)


def kernel(secs, strips, feat, offsets, w_one, b_one, w_two, b_two, w_three, out,
           mine, wide, corr, hid_one, hid_two, wide_one, wide_two, send_sem, recv_sem):
    rows, cols, chans = feat.shape[1:]
    hid = b_one.shape[1]
    planes = w_one.shape[2]
    depth = corr.shape[2]
    sec, strip = lax.axis_index("sec"), lax.axis_index("strip")

    for d in range(3):
        for e in range(3):
            if planes < depth:
                wide_one[d * depth:(d + 1) * depth, (2 - e) * hid:(3 - e) * hid] = jnp.zeros((depth, hid), wide_one.dtype)
            wide_one[d * depth:d * depth + planes, (2 - e) * hid:(3 - e) * hid] = w_one[d, e]
            wide_two[d * hid:(d + 1) * hid, (2 - e) * hid:(3 - e) * hid] = w_two[d, e]

    exchange(secs, strips, feat, mine, wide, send_sem, recv_sem)

    shifts = (
        jnp.where(sec > 0, -offsets[jnp.maximum(sec - 1, 0)], 0),
        jnp.where(sec < secs - 1, offsets[sec], 0),
    )
    scale = chans ** (-0.5)
    lane = lax.broadcasted_iota(jnp.int32, (cols, cols), 1)
    col = lax.broadcasted_iota(jnp.int32, (cols, cols), 0)
    flip = (lane + col == cols - 1).astype(mine.dtype)
    gains = []
    for tile in range(depth // cols):
        plane = lane + tile * cols
        other = cols - 1 - col + lax.rem(plane, TAPS) - 4
        gains.append(jnp.where((other >= 0) & (other < cols) & (plane < planes), scale, 0.0))

    def correlate(r, carry):
        here = jnp.dot(flip, mine[r], preferred_element_type=jnp.float32).astype(mine.dtype)
        found = [jnp.zeros((cols, cols), jnp.float32) for _ in gains]
        for j in range(2):
            there = wide[j, pl.ds(r + 2 + shifts[j], TAPS)].reshape(TAPS * cols, chans)
            products = lax.dot_general(here, there, (((1,), (1,)), ((), ())), preferred_element_type=jnp.float32)
            for a in range(TAPS):
                first = (j * TAPS + a) * TAPS
                turned = skewed(products[:, a * cols:(a + 1) * cols], first + 5)
                for tile in range(len(gains)):
                    low = first - tile * cols
                    if low < cols and low + TAPS > 0:
                        found[tile] = jnp.where((lane >= low) & (lane < low + TAPS), turned, found[tile])
        for tile, gain in enumerate(gains):
            corr[r, :, tile * cols:(tile + 1) * cols] = (found[tile] * gain).astype(corr.dtype)
        return carry

    lax.fori_loop(0, rows + 6, correlate, 0)

    convolve(corr, wide_one, b_one, hid_one)

    @pl.when(strip == 0)
    def _():
        hid_one[0:2] = jnp.zeros((2, cols, hid), hid_one.dtype)

    @pl.when(strip == strips - 1)
    def _():
        hid_one[rows + 2:] = jnp.zeros((2, cols, hid), hid_one.dtype)

    convolve(hid_one, wide_two, b_two, hid_two)

    @pl.when(strip == 0)
    def _():
        hid_two[0:1] = jnp.zeros((1, cols, hid), hid_two.dtype)

    @pl.when(strip == strips - 1)
    def _():
        hid_two[rows + 1:] = jnp.zeros((1, cols, hid), hid_two.dtype)

    taps = lax.dot_general(
        w_three[...], hid_two[...].reshape((rows + 2) * cols, hid), (((1,), (1,)), ((), ())),
        preferred_element_type=jnp.float32,
    )
    at_lane = lax.broadcasted_iota(jnp.int32, (8, cols), 1)
    found = []
    for r in range(rows):
        total = sum(taps[8 * d:8 * d + 8, (r + d) * cols:(r + d + 1) * cols] for d in range(3))
        before = jnp.where(at_lane == 0, 0.0, pltpu.roll(total, 1, 1))
        after = jnp.where(at_lane == cols - 1, 0.0, pltpu.roll(total, cols - 1, 1))
        found.append(before[0:2] + total[2:4] + after[4:6])
    turned = jnp.dot(
        jnp.concatenate(found, axis=0), flip.astype(jnp.float32),
        preferred_element_type=jnp.float32, precision=lax.Precision.HIGHEST,
    )
    for r in range(rows):
        out[:, r, :] = turned[2 * r:2 * r + 2]


def body(secs, strips, features, offsets, state, w_first, b_first, w_second, b_second, w_third):
    _, rows, cols, chans = features.shape
    planes, hid = w_first.shape[2:]
    depth = -(-planes // cols) * cols
    parts = w_third.shape[3]
    thirds = jnp.pad(jnp.transpose(w_third[:, ::-1], (0, 1, 3, 2)).reshape(3, 3 * parts, hid), ((0, 0), (0, 8 - 3 * parts), (0, 0)))
    copies = 2 * (rows // STEP) + 4 * (SIDE // STEP) + 2
    bf16 = jnp.bfloat16
    delta = pl.pallas_call(
        functools.partial(kernel, secs, strips),
        out_shape=jax.ShapeDtypeStruct((parts, rows, cols), jnp.float32),
        in_specs=[VMEM, SMEM] + [VMEM] * 5,
        out_specs=VMEM,
        scratch_shapes=[
            pltpu.VMEM((rows + 6, cols, chans), bf16),
            pltpu.VMEM((2, rows + 2 * SIDE, cols, chans), bf16),
            pltpu.VMEM((rows + 6, cols, depth), bf16),
            pltpu.VMEM((rows + 4, cols, hid), bf16),
            pltpu.VMEM((rows + 2, cols, hid), bf16),
            pltpu.VMEM((3 * depth, 3 * hid), bf16),
            pltpu.VMEM((3 * hid, 3 * hid), bf16),
            pltpu.SemaphoreType.DMA((copies,)),
            pltpu.SemaphoreType.DMA((copies,)),
        ],
        compiler_params=pltpu.CompilerParams(collective_id=0, has_side_effects=True, vmem_limit_bytes=48 << 20),
    )(features, offsets, w_first, b_first.reshape(1, hid), w_second, b_second.reshape(1, hid), thirds.reshape(24, hid))
    return state + delta[:, None]


def solution(mesh):
    secs, strips = mesh.shape["sec"], mesh.shape["strip"]
    in_specs = (
        P("sec", "strip", None, None),
        P(),
        P(None, "sec", "strip", None),
        P(),
        P(),
        P(),
        P(),
        P(),
    )
    out_specs = P(None, "sec", "strip", None)
    return jax.shard_map(functools.partial(body, secs, strips), mesh=mesh, in_specs=in_specs, out_specs=out_specs, check_vma=False)
```

time: 111 us -> 41.6 us (0.37)
  the two profiles are of different devices: /device:TPU:18 before, /device:TPU:13 now
where the time goes in v1:
time: 41.6 us; the launch traced here: 41.4 us
  Pallas kernels  36.3 us (87%)
  local copies, waits for them, and re-layouts  4.94 us (12%)
    pallas_call x1, Pallas kernels, body(): pl.pallas_call(functools.partial(kernel, secs, strips), out_shape=jax.Sha...  36.3 us
    unnamed x14, local copies, waits for them, and re-layouts  3.6 us

profile of v1, /device:TPU:13, one launch (start us, length us, event | category | flops | bytes accessed | tf_op | source)
XLA Modules:
  0.0 41.4 jit_solution(17959527190346458775)
XLA Ops:
  0.0 0.7 %reverse_bitcast_fusion = bf16[3,3,2,128]{3,2,1,0:T(2,128)(2,1)S(1)} fusion(bf16[3,3,128,2]{2,3,1,0:T(2,128)(2,1)} %param.15), kind=kLoop, calls=%fused_computation.2 | loop fusion | bytes 9216 | tf_op jit(solution)/shard_map/transpose | solution.py:268
  0.7 0.0 copy-start.3
  0.7 0.0 copy-start.4
  0.7 0.0 copy-start.5
  0.8 0.6 %copy-done.3 = s32[4]{0:T(128)S(1)} copy-done((s32[4]{0:T(128)S(1)}, s32[4]{0:T(128)}, u32[]{:S(2)}) %copy-start.3) | copy-done | bytes 40
  1.4 0.0 copy-done.4
  1.4 0.0 copy-done.5
  1.4 0.0 copy-start
  1.4 1.0 %copy-done = bf16[1,12,128,128]{3,2,1,0:T(8,128)(2,1)S(1)} copy-done((bf16[1,12,128,128]{3,2,1,0:T(8,128)(2,1)S(1)}, bf16[1,12,128,128]{3,2,1,0:T(8,128)(2,1)}, u32[]{:S(2)}) %copy-start) | copy-done | bytes 393240
  2.4 0.0 copy-start.1
  2.4 1.0 %copy-done.1 = bf16[3,3,162,128]{3,2,1,0:T(8,128)(2,1)S(1)} copy-done((bf16[3,3,162,128]{3,2,1,0:T(8,128)(2,1)S(1)}, bf16[3,3,162,128]{3,2,1,0:T(8,128)(2,1)}, u32[]{:S(2)}) %copy-start.1) | copy-done | bytes 373272
  3.4 0.0 copy-start.2
  3.4 1.0 %copy-done.2 = bf16[3,3,128,128]{3,2,1,0:T(8,128)(2,1)S(1)} copy-done((bf16[3,3,128,128]{3,2,1,0:T(8,128)(2,1)S(1)}, bf16[3,3,128,128]{3,2,1,0:T(8,128)(2,1)}, u32[]{:S(2)}) %copy-start.2) | copy-done | bytes 294936
  4.4 0.0 copy-start.6
  4.4 36.3 %shard_map.82 = f32[2,12,128]{2,1,0:T(8,128)S(1)} custom-call(bf16[1,12,128,128]{3,2,1,0:T(8,128)(2,1)S(1)} %copy-done, s32[4]{0:T(128)S(1)} %copy-done.3, bf16[3,3,162,128]{3,2,1,0:T(8,128)(2,1)S(1)} %copy-done.1, f32[1,128]{1,0:T(1,128)S(1)} %bitcast.8, bf16[3,3,128,128]{3,2,1,0:T(8,128)(2,1)S(1)} %copy-done.2, f32[1,128]{1,0:T(1,128)S(1)} %bitcast.9, ...), custom_call_target="tpu_custom_call" | custom-call | tf_op jit(solution)/shard_map/pallas_call | solution.py:271
  40.7 0.0 copy-done.6
  40.7 0.6 %copy.10 = f32[2,1,12,128]{3,1,2,0:T(1,128)} copy(f32[2,1,12,128]{3,2,0,1:T(8,128)S(1)} %bitcast_add_fusion) | data formatting | bytes 24576 | tf_op jit(solution)/shard_map/add | solution.py:289
  (3 shorter events, 0.0 us)
Async XLA Ops:
  0.7 0.7 %copy-start.3 = (s32[4]{0:T(128)S(1)}, s32[4]{0:T(128)}, u32[]{:S(2)}) copy-start(s32[4]{0:T(128)} %offsets.1) | copy-start | bytes 52
  0.7 0.7 %copy-start.4 = (f32[128]{0:T(128)S(1)}, f32[128]{0:T(128)}, u32[]{:S(2)}) copy-start(f32[128]{0:T(128)} %param.12) | copy-start | bytes 1540
  0.7 0.7 %copy-start.5 = (f32[128]{0:T(128)S(1)}, f32[128]{0:T(128)}, u32[]{:S(2)}) copy-start(f32[128]{0:T(128)} %param.14) | copy-start | bytes 1540
  1.4 1.0 %copy-start = (bf16[1,12,128,128]{3,2,1,0:T(8,128)(2,1)S(1)}, bf16[1,12,128,128]{3,2,1,0:T(8,128)(2,1)}, u32[]{:S(2)}) copy-start(bf16[1,12,128,128]{3,2,1,0:T(8,128)(2,1)} %feat.1) | copy-start | bytes 1179652
  2.4 1.0 %copy-start.1 = (bf16[3,3,162,128]{3,2,1,0:T(8,128)(2,1)S(1)}, bf16[3,3,162,128]{3,2,1,0:T(8,128)(2,1)}, u32[]{:S(2)}) copy-start(bf16[3,3,162,128]{3,2,1,0:T(8,128)(2,1)} %w_one.1) | copy-start | bytes 1119748
  3.4 1.0 %copy-start.2 = (bf16[3,3,128,128]{3,2,1,0:T(8,128)(2,1)S(1)}, bf16[3,3,128,128]{3,2,1,0:T(8,128)(2,1)}, u32[]{:S(2)}) copy-start(bf16[3,3,128,128]{3,2,1,0:T(8,128)(2,1)} %w_two.1) | copy-start | bytes 884740
  4.4 36.4 %copy-start.6 = (f32[2,1,12,128]{3,1,2,0:T(1,128)S(1)}, f32[2,1,12,128]{3,1,2,0:T(1,128)}, u32[]{:S(2)}) copy-start(f32[2,1,12,128]{3,1,2,0:T(1,128)} %param.10) | copy-start | bytes 36868

commit v2 on v1

v2 whole, which is shorter than its diff:
```python
import functools

import jax
import jax.numpy as jnp
from jax import lax
from jax.experimental import pallas as pl
from jax.experimental.pallas import tpu as pltpu
from jax.sharding import PartitionSpec as P

SIDE = 9
STEP = 3
TAPS = 9
VMEM = pl.BlockSpec(memory_space=pltpu.VMEM)
HBM = pl.BlockSpec(memory_space=pltpu.HBM)
SMEM = pl.BlockSpec(memory_space=pltpu.SMEM)


def group_of(rows):
    return max(g for g in range(1, 8) if rows % g == 0)


def exchange(secs, strips, feat, mine, near, far, send_sem, recv_sem, loads, prepare, turn, relate):
    rows = feat.shape[1]
    count = rows // STEP
    sec, strip = lax.axis_index("sec"), lax.axis_index("strip")
    odd = lax.rem(sec, 2)
    partner = sec + 1 - 2 * odd
    relay_to, relay_from = sec + 2 - 4 * odd, sec - 2 + 4 * odd
    has_to = (relay_to >= 0) & (relay_to < secs)
    has_from = (relay_from >= 0) & (relay_from < secs)
    has_low, has_high = strip > 0, strip < strips - 1

    barrier = pltpu.get_barrier_semaphore()
    greeted = (
        (None, partner, strip),
        (has_to, relay_to, strip),
        (has_from, relay_from, strip),
        (has_low, sec, strip - 1),
        (has_high, sec, strip + 1),
    )

    def when(cond, act):
        if cond is None:
            act()
        else:
            pl.when(cond)(act)

    for cond, a, b in greeted:
        when(cond, lambda a=a, b=b: pl.semaphore_signal(barrier, inc=1, device_id=(a, b), device_id_type=pl.DeviceIdType.MESH))

    for load in loads:
        load.start()
    pl.semaphore_wait(barrier, 1 + sum(cond.astype(jnp.int32) for cond, _, _ in greeted[1:]))

    waits = []
    number = [0]

    def copy(src, dst, a, b, sends, gets):
        at = number[0]
        number[0] += 1
        made = pltpu.make_async_remote_copy(
            src_ref=src, dst_ref=dst, send_sem=send_sem.at[at], recv_sem=recv_sem.at[at],
            device_id=(a, b), device_id_type=pl.DeviceIdType.MESH,
        )
        when(sends, made.start)
        waits.append((sends, made.wait_send))
        return lambda: when(gets, made.wait_recv)

    def both(x, y):
        return y if x is None else x & y

    def down(slot, q, known):
        return copy(
            slot.at[pl.ds(SIDE + STEP * q, STEP)], slot.at[pl.ds(SIDE + rows + STEP * q, STEP)],
            sec, strip - 1, both(known, has_low), both(known, has_high),
        )

    def up(slot, q, known):
        return copy(
            slot.at[pl.ds(SIDE + STEP * q, STEP)], slot.at[pl.ds(SIDE + STEP * q - rows, STEP)],
            sec, strip + 1, both(known, has_high), both(known, has_low),
        )

    order = list(range(count))
    direct = [
        copy(feat.at[0, pl.ds(STEP * q, STEP)], near.at[pl.ds(SIDE + STEP * q, STEP)], partner, strip, None, None)
        for q in order
    ]
    last = []
    last.append(copy(feat.at[0, pl.ds(0, STEP)], mine.at[pl.ds(STEP + rows, STEP)], sec, strip - 1, has_low, has_high))
    last.append(copy(feat.at[0, pl.ds(rows - STEP, STEP)], mine.at[pl.ds(0, STEP)], sec, strip + 1, has_high, has_low))

    zero = jnp.zeros((SIDE,) + near.shape[1:], near.dtype)

    @pl.when(jnp.logical_not(has_from))
    def _():
        far[...] = jnp.zeros(far.shape, far.dtype)

    @pl.when(jnp.logical_not(has_low))
    def _():
        near[0:SIDE] = zero
        far[0:SIDE] = zero
        mine[0:STEP] = zero[:STEP]

    @pl.when(jnp.logical_not(has_high))
    def _():
        near[SIDE + rows:] = zero
        far[SIDE + rows:] = zero
        mine[STEP + rows:] = zero[:STEP]

    prepare()
    for wait in last:
        wait()
    turn()
    relayed = []
    ends = ([], [])

    def sides(slot, q, known, found):
        if STEP * q < SIDE:
            found.append(down(slot, q, known))
        if STEP * q >= rows - SIDE:
            found.append(up(slot, q, known))

    for q in order + [count]:
        if q < count:
            direct[q]()
            relayed.append(copy(
                near.at[pl.ds(SIDE + STEP * q, STEP)], far.at[pl.ds(SIDE + STEP * q, STEP)],
                relay_to, strip, has_to, has_from,
            ))
            sides(near, q, None, ends[0])
        if q >= 1:
            relayed[q - 1]()
            sides(far, q - 1, has_from, ends[1])
    for wide, found, slot in zip((near, far), ends, (1 - odd, odd)):
        for wait in found:
            wait()
        relate(wide, slot)
    for cond, wait in waits:
        when(cond, wait)


def convolve(sources, weight, bias, target):
    rows, cols, width = target.shape
    depth = sources[0].shape[2]
    group = group_of(rows)
    at_col = lax.broadcasted_iota(jnp.int32, (cols, width), 0)

    def step(g, carry):
        base = g * group
        taken = jnp.concatenate(
            [s[pl.ds(base + d, group)].reshape(group * cols, depth) for d in range(3) for s in sources], axis=1
        )
        sums = jnp.dot(taken, weight[...], preferred_element_type=jnp.float32)
        for i in range(group):
            one = sums[i * cols:(i + 1) * cols]
            before = jnp.where(at_col == 0, 0.0, pltpu.roll(one[:, :width], 1, 0))
            after = jnp.where(at_col == cols - 1, 0.0, pltpu.roll(one[:, 2 * width:], cols - 1, 0))
            total = one[:, width:2 * width] + before + after + bias[...]
            target[base + i] = jnp.maximum(total, 0.0).astype(target.dtype)
        return carry

    lax.fori_loop(0, rows // group, step, 0)


def skewed(block, shift):
    rows, cols = block.shape
    pieces = []
    start = 0
    for top in range(0, rows, 8):
        if (shift + top) % cols + 7 > cols:
            if top > start:
                pieces.append(pltpu.roll(block[start:top], (shift + start) % cols, 1, stride=1, stride_axis=0))
            crossing = pltpu.roll(block[top:top + 8], (shift + top - 8) % cols, 1, stride=1, stride_axis=0)
            pieces.append(pltpu.roll(crossing, 8, 1))
            start = top + 8
    if start < rows:
        pieces.append(pltpu.roll(block[start:], (shift + start) % cols, 1, stride=1, stride_axis=0))
    return jnp.concatenate(pieces, axis=0)


def kernel(secs, strips, feat, offsets, w_one, b_one, w_two, b_two, w_three, out,
           mine, near, far, corr, hid_one, hid_two, held_one, held_two, wide_one, wide_two, thirds,
           send_sem, recv_sem, local_sem):
    rows, cols, chans = feat.shape[1:]
    hid = b_one.shape[1]
    planes = w_one.shape[2] // 2
    sec, strip = lax.axis_index("sec"), lax.axis_index("strip")
    loads = [
        pltpu.make_async_copy(feat.at[0], mine.at[pl.ds(STEP, rows)], local_sem.at[0]),
        pltpu.make_async_copy(w_one, held_one, local_sem.at[1]),
        pltpu.make_async_copy(w_two, held_two, local_sem.at[2]),
    ]

    def prepare():
        for d in range(3):
            thirds[8 * d:8 * d + 8] = jnp.zeros((8, hid), thirds.dtype)
            for e in range(3):
                thirds[8 * d + 4 - 2 * e:8 * d + 6 - 2 * e] = w_three[d, e].astype(thirds.dtype)
        for d in range(2 * 3):
            wide_one[d * cols + planes // 16 * 16:(d + 1) * cols] = jnp.zeros((cols - planes // 16 * 16, 3 * hid), wide_one.dtype)
        loads[1].wait()
        loads[2].wait()
        for d in range(3):
            for e in range(3):
                at = pl.ds((2 - e) * hid, hid)
                for j in range(2):
                    wide_one[pl.ds((2 * d + j) * cols, planes), at] = held_one[d, e, j * planes:(j + 1) * planes]
                wide_two[pl.ds(d * hid, hid), at] = held_two[d, e]
        loads[0].wait()

    scale = chans ** (-0.5)
    lane = lax.broadcasted_iota(jnp.int32, (cols, cols), 1)
    col = lax.broadcasted_iota(jnp.int32, (cols, cols), 0)
    flip = (lane + col == cols - 1).astype(mine.dtype)
    other = cols - 1 - col + lax.rem(lane, TAPS) - 4
    gain = jnp.where((other >= 0) & (other < cols) & (lane < planes), scale, 0.0)
    shifts = (
        jnp.where(sec > 0, -offsets[jnp.maximum(sec - 1, 0)], 0),
        jnp.where(sec < secs - 1, offsets[sec], 0),
    )

    def turn():
        def one(r, carry):
            mine[r] = jnp.dot(flip, mine[r], preferred_element_type=jnp.float32).astype(mine.dtype)
            return carry

        lax.fori_loop(0, rows + 6, one, 0)

    group = 6 if rows % 6 == 0 else 2

    def relate(wide, slot):
        shift = jnp.where(slot == 0, shifts[0], shifts[1])

        def step(g, carry):
            base = g * group
            here = mine[pl.ds(base, group)].reshape(group * cols, chans)
            products = {}
            for t in range(0, group + TAPS - 1, 2):
                low, high = max(0, t - TAPS + 1), min(group, t + 2)
                there = wide[pl.ds(base + 2 + shift + t, 2)].reshape(2 * cols, chans)
                tile = lax.dot_general(
                    here[low * cols:high * cols], there, (((1,), (1,)), ((), ())), preferred_element_type=jnp.float32
                )
                for i in range(low, high):
                    for u in range(2):
                        if 0 <= t + u - i < TAPS:
                            products[i, t + u - i] = tile[(i - low) * cols:(i - low + 1) * cols, u * cols:(u + 1) * cols]
            for i in range(group):
                found = skewed(products[i, 0], 5)
                for a in range(1, TAPS):
                    found = jnp.where(lane >= a * TAPS, skewed(products[i, a], a * TAPS + 5), found)
                corr[slot, base + i] = (found * gain).astype(corr.dtype)
            return carry

        lax.fori_loop(0, (rows + 6) // group, step, 0)

    exchange(secs, strips, feat, mine, near, far, send_sem, recv_sem, loads, prepare, turn, relate)

    convolve((corr.at[0], corr.at[1]), wide_one, b_one, hid_one)

    @pl.when(strip == 0)
    def _():
        hid_one[0:2] = jnp.zeros((2, cols, hid), hid_one.dtype)

    @pl.when(strip == strips - 1)
    def _():
        hid_one[rows + 2:] = jnp.zeros((2, cols, hid), hid_one.dtype)

    convolve((hid_one,), wide_two, b_two, hid_two)

    @pl.when(strip == 0)
    def _():
        hid_two[0:1] = jnp.zeros((1, cols, hid), hid_two.dtype)

    @pl.when(strip == strips - 1)
    def _():
        hid_two[rows + 1:] = jnp.zeros((1, cols, hid), hid_two.dtype)

    taps = lax.dot_general(
        thirds[...].astype(hid_two.dtype), hid_two[...].reshape((rows + 2) * cols, hid), (((1,), (1,)), ((), ())),
        preferred_element_type=jnp.float32,
    )
    at_lane = lax.broadcasted_iota(jnp.int32, (8, cols), 1)
    found = []
    for r in range(rows):
        total = sum(taps[8 * d:8 * d + 8, (r + d) * cols:(r + d + 1) * cols] for d in range(3))
        before = jnp.where(at_lane == 0, 0.0, pltpu.roll(total, 1, 1))
        after = jnp.where(at_lane == cols - 1, 0.0, pltpu.roll(total, cols - 1, 1))
        found.append(before[0:2] + total[2:4] + after[4:6])
    turned = jnp.dot(
        jnp.concatenate(found, axis=0), flip.astype(jnp.float32),
        preferred_element_type=jnp.float32, precision=lax.Precision.HIGHEST,
    )
    for r in range(rows):
        out[:, r, :] = turned[2 * r:2 * r + 2]


def body(secs, strips, features, offsets, state, w_first, b_first, w_second, b_second, w_third):
    _, rows, cols, chans = features.shape
    hid = w_first.shape[3]
    parts = w_third.shape[3]
    copies = 2 * (rows // STEP) + 4 * (SIDE // STEP) + 2
    bf16 = jnp.bfloat16
    delta = pl.pallas_call(
        functools.partial(kernel, secs, strips),
        out_shape=jax.ShapeDtypeStruct((parts, rows, cols), jnp.float32),
        in_specs=[HBM, SMEM, HBM, VMEM, HBM, VMEM, VMEM],
        out_specs=VMEM,
        scratch_shapes=[
            pltpu.VMEM((rows + 6, cols, chans), bf16),
            pltpu.VMEM((rows + 2 * SIDE, cols, chans), bf16),
            pltpu.VMEM((rows + 2 * SIDE, cols, chans), bf16),
            pltpu.VMEM((2, rows + 6, cols, cols), bf16),
            pltpu.VMEM((rows + 4, cols, hid), bf16),
            pltpu.VMEM((rows + 2, cols, hid), bf16),
            pltpu.VMEM(w_first.shape, bf16),
            pltpu.VMEM(w_second.shape, bf16),
            pltpu.VMEM((6 * cols, 3 * hid), bf16),
            pltpu.VMEM((3 * hid, 3 * hid), bf16),
            pltpu.VMEM((24, hid), jnp.float32),
            pltpu.SemaphoreType.DMA((copies,)),
            pltpu.SemaphoreType.DMA((copies,)),
            pltpu.SemaphoreType.DMA((3,)),
        ],
        compiler_params=pltpu.CompilerParams(collective_id=0, has_side_effects=True, vmem_limit_bytes=56 << 20),
    )(
        features, offsets, w_first, b_first.reshape(1, hid), w_second, b_second.reshape(1, hid),
        jnp.transpose(w_third, (0, 1, 3, 2)),
    )
    return state + delta[:, None]


def solution(mesh):
    secs, strips = mesh.shape["sec"], mesh.shape["strip"]
    in_specs = (
        P("sec", "strip", None, None),
        P(),
        P(None, "sec", "strip", None),
        P(),
        P(),
        P(),
        P(),
        P(),
    )
    out_specs = P(None, "sec", "strip", None)
    return jax.shard_map(functools.partial(body, secs, strips), mesh=mesh, in_specs=in_specs, out_specs=out_specs, check_vma=False)
```

time: 41.6 us -> 35.1 us (0.84)
  the two profiles are of different devices: /device:TPU:13 before, /device:TPU:18 now
where the time goes in v2:
time: 35.1 us; the launch traced here: 34.5 us
  Pallas kernels  33.1 us (94%)
  other arithmetic  0.72 us (2%)
  local copies, waits for them, and re-layouts  0.62 us (2%)
    pallas_call x1, Pallas kernels, body(): pl.pallas_call(functools.partial(kernel, secs, strips), out_shape=jax.Sha...  33.1 us
    add x1, other arithmetic, body(): return state + delta[:, None]  0.72 us

profile of v2, /device:TPU:18, one launch (start us, length us, event | category | flops | bytes accessed | tf_op | source)
XLA Modules:
  0.0 34.5 jit_solution(9077076292853239703)
XLA Ops:
  0.0 0.0 copy-start
  0.0 33.1 %shard_map.82 = f32[2,12,128]{2,1,0:T(8,128)} custom-call(bf16[1,12,128,128]{3,2,1,0:T(8,128)(2,1)} %feat.1, s32[4]{0:T(128)} %offsets.1, bf16[3,3,162,128]{3,2,1,0:T(8,128)(2,1)} %w_one.1, f32[1,128]{1,0:T(1,128)} %bitcast.6, bf16[3,3,128,128]{3,2,1,0:T(8,128)(2,1)} %w_two.1, f32[1,128]{1,0:T(1,128)} %bitcast.7, bf16[3,3,2,128]{3,2,1,0:T(2,128)(2,1)} %bitcast.5), custom_call_target="tpu_custom_call" | custom-call | tf_op jit(solution)/shard_map/pallas_call | solution.py:305
  33.1 0.0 copy-done
  33.1 0.7 %bitcast_add_fusion = f32[2,1,12,128]{3,2,0,1:T(8,128)S(1)} fusion(f32[2,12,128]{2,1,0:T(8,128)} %shard_map.82, f32[2,1,12,128]{3,1,2,0:T(1,128)S(1)} %copy-done), kind=kLoop, calls=%fused_computation | loop fusion | flops 3072 | bytes 36864 | tf_op jit(solution)/shard_map/add | solution.py:331
  33.8 0.6 %copy.10 = f32[2,1,12,128]{3,1,2,0:T(1,128)} copy(f32[2,1,12,128]{3,2,0,1:T(8,128)S(1)} %bitcast_add_fusion) | data formatting | bytes 24576 | tf_op jit(solution)/shard_map/add | solution.py:331
Async XLA Ops:
  0.0 33.1 %copy-start = (f32[2,1,12,128]{3,1,2,0:T(1,128)S(1)}, f32[2,1,12,128]{3,1,2,0:T(1,128)}, u32[]{:S(2)}) copy-start(f32[2,1,12,128]{3,1,2,0:T(1,128)} %param.10) | copy-start | bytes 36868

commit v3 on v2

--- a/solution.py
+++ b/solution.py
@@ -9,6 +9,7 @@
 
 SIDE = 9
 STEP = 3
+PIECE = STEP
 TAPS = 9
 VMEM = pl.BlockSpec(memory_space=pltpu.VMEM)
 HBM = pl.BlockSpec(memory_space=pltpu.HBM)
@@ -21,7 +22,7 @@
 
 def exchange(secs, strips, feat, mine, near, far, send_sem, recv_sem, loads, prepare, turn, relate):
     rows = feat.shape[1]
-    count = rows // STEP
+    count = rows // PIECE
     sec, strip = lax.axis_index("sec"), lax.axis_index("strip")
     odd = lax.rem(sec, 2)
     partner = sec + 1 - 2 * odd
@@ -71,19 +72,19 @@
 
     def down(slot, q, known):
         return copy(
-            slot.at[pl.ds(SIDE + STEP * q, STEP)], slot.at[pl.ds(SIDE + rows + STEP * q, STEP)],
+            slot.at[pl.ds(SIDE + PIECE * q, PIECE)], slot.at[pl.ds(SIDE + rows + PIECE * q, PIECE)],
             sec, strip - 1, both(known, has_low), both(known, has_high),
         )
 
     def up(slot, q, known):
         return copy(
-            slot.at[pl.ds(SIDE + STEP * q, STEP)], slot.at[pl.ds(SIDE + STEP * q - rows, STEP)],
+            slot.at[pl.ds(SIDE + PIECE * q, PIECE)], slot.at[pl.ds(SIDE + PIECE * q - rows, PIECE)],
             sec, strip + 1, both(known, has_high), both(known, has_low),
         )
 
     order = list(range(count))
     direct = [
-        copy(feat.at[0, pl.ds(STEP * q, STEP)], near.at[pl.ds(SIDE + STEP * q, STEP)], partner, strip, None, None)
+        copy(feat.at[0, pl.ds(PIECE * q, PIECE)], near.at[pl.ds(SIDE + PIECE * q, PIECE)], partner, strip, None, None)
         for q in order
     ]
     last = []
@@ -108,30 +109,32 @@
         far[SIDE + rows:] = zero
         mine[STEP + rows:] = zero[:STEP]
 
-    prepare()
-    for wait in last:
-        wait()
-    turn()
     relayed = []
     ends = ([], [])
 
     def sides(slot, q, known, found):
-        if STEP * q < SIDE:
+        if PIECE * q < SIDE:
             found.append(down(slot, q, known))
-        if STEP * q >= rows - SIDE:
+        if PIECE * q >= rows - SIDE:
             found.append(up(slot, q, known))
 
     for q in order + [count]:
         if q < count:
             direct[q]()
             relayed.append(copy(
-                near.at[pl.ds(SIDE + STEP * q, STEP)], far.at[pl.ds(SIDE + STEP * q, STEP)],
+                near.at[pl.ds(SIDE + PIECE * q, PIECE)], far.at[pl.ds(SIDE + PIECE * q, PIECE)],
                 relay_to, strip, has_to, has_from,
             ))
             sides(near, q, None, ends[0])
         if q >= 1:
             relayed[q - 1]()
             sides(far, q - 1, has_from, ends[1])
+        if q == count // 4:
+            prepare()
+        if q == count // 2:
+            for wait in last:
+                wait()
+            turn()
     for wide, found, slot in zip((near, far), ends, (1 - odd, odd)):
         for wait in found:
             wait()
@@ -293,18 +296,19 @@
         preferred_element_type=jnp.float32, precision=lax.Precision.HIGHEST,
     )
     for r in range(rows):
-        out[:, r, :] = turned[2 * r:2 * r + 2]
+        for p in range(2):
+            out[p * rows + r] = turned[2 * r + p:2 * r + p + 1]
 
 
 def body(secs, strips, features, offsets, state, w_first, b_first, w_second, b_second, w_third):
     _, rows, cols, chans = features.shape
     hid = w_first.shape[3]
     parts = w_third.shape[3]
-    copies = 2 * (rows // STEP) + 4 * (SIDE // STEP) + 2
+    copies = 2 * (rows // PIECE) + 4 * (SIDE // PIECE) + 2
     bf16 = jnp.bfloat16
     delta = pl.pallas_call(
         functools.partial(kernel, secs, strips),
-        out_shape=jax.ShapeDtypeStruct((parts, rows, cols), jnp.float32),
+        out_shape=jax.ShapeDtypeStruct((parts * rows, 1, cols), jnp.float32),
         in_specs=[HBM, SMEM, HBM, VMEM, HBM, VMEM, VMEM],
         out_specs=VMEM,
         scratch_shapes=[
@@ -328,7 +332,7 @@
         features, offsets, w_first, b_first.reshape(1, hid), w_second, b_second.reshape(1, hid),
         jnp.transpose(w_third, (0, 1, 3, 2)),
     )
-    return state + delta[:, None]
+    return state + delta.reshape(state.shape)
 
 
 def solution(mesh):

time: 35.1 us -> 33.2 us (0.946); the launches traced: 34.5 us -> 32.9 us
  Pallas kernels: 33.1 us -> 31.6 us
  local copies, waits for them, and re-layouts: 0.62 us -> 0.01 us
  other arithmetic: 0.72 us -> 1.32 us
    pallas_call x1, Pallas kernels: 33.1 us -> 31.6 us  [body(): pl.pallas_call(functools.partial(kernel, secs, strips), out_shape=jax.Sha...]
    add x1 -> x0, local copies, waits for them, and re-layouts: 0.61 us -> none  [body(): return state + delta[:, None]]
    add x1, other arithmetic: 0.72 us -> 1.32 us  [body(): return state + delta.reshape(state.shape)]
where the time goes in v3:
time: 33.2 us; the launch traced here: 32.9 us
  Pallas kernels  31.6 us (95%)
  other arithmetic  1.32 us (4%)
    pallas_call x1, Pallas kernels, body(): pl.pallas_call(functools.partial(kernel, secs, strips), out_shape=jax.Sha...  31.6 us
    add x1, other arithmetic, body(): return state + delta.reshape(state.shape)  1.32 us

profile of v3, /device:TPU:18, one launch (start us, length us, event | category | flops | bytes accessed | tf_op | source)
XLA Modules:
  0.0 32.9 jit_solution(5273156049440848343)
XLA Ops:
  0.0 0.0 copy-start
  0.0 31.6 %shard_map.82 = f32[24,1,128]{2,1,0:T(1,128)} custom-call(bf16[1,12,128,128]{3,2,1,0:T(8,128)(2,1)} %feat.1, s32[4]{0:T(128)} %offsets.1, bf16[3,3,162,128]{3,2,1,0:T(8,128)(2,1)} %w_one.1, f32[1,128]{1,0:T(1,128)} %bitcast.6, bf16[3,3,128,128]{3,2,1,0:T(8,128)(2,1)} %w_two.1, f32[1,128]{1,0:T(1,128)} %bitcast.7, bf16[3,3,2,128]{3,2,1,0:T(2,128)(2,1)} %bitcast.5), custom_call_target="tpu_custom_call" | custom-call | tf_op jit(solution)/shard_map/pallas_call | solution.py:309
  31.6 0.0 copy-done
  31.6 1.3 %add.3 = f32[2,1,12,128]{3,1,2,0:T(1,128)} add(f32[2,1,12,128]{3,1,2,0:T(1,128)S(1)} %copy-done, f32[2,1,12,128]{3,1,2,0:T(1,128)} %bitcast.4) | non-fusion elementwise | flops 3072 | bytes 36864 | tf_op jit(solution)/shard_map/add | solution.py:335
Async XLA Ops:
  0.0 31.6 %copy-start = (f32[2,1,12,128]{3,1,2,0:T(1,128)S(1)}, f32[2,1,12,128]{3,1,2,0:T(1,128)}, u32[]{:S(2)}) copy-start(f32[2,1,12,128]{3,1,2,0:T(1,128)} %param.10) | copy-start | bytes 36868

commit v4 on v3

--- a/solution.py
+++ b/solution.py
@@ -20,7 +20,7 @@
     return max(g for g in range(1, 8) if rows % g == 0)
 
 
-def exchange(secs, strips, feat, mine, near, far, send_sem, recv_sem, loads, prepare, turn, relate):
+def exchange(secs, strips, feat, mine, near, far, send_sem, recv_sem, loads, prepare, turn, own, relate):
     rows = feat.shape[1]
     count = rows // PIECE
     sec, strip = lax.axis_index("sec"), lax.axis_index("strip")
@@ -135,9 +135,13 @@
             for wait in last:
                 wait()
             turn()
+            own(near, 1 - odd, 0, rows // 4)
+    own(near, 1 - odd, rows // 4, rows // 2)
     for wide, found, slot in zip((near, far), ends, (1 - odd, odd)):
         for wait in found:
             wait()
+        if wide is far:
+            own(far, odd, 0, rows // 2)
         relate(wide, slot)
     for cond, wait in waits:
         when(cond, wait)
@@ -183,7 +187,7 @@
 
 
 def kernel(secs, strips, feat, offsets, w_one, b_one, w_two, b_two, w_three, out,
-           mine, near, far, corr, hid_one, hid_two, held_one, held_two, wide_one, wide_two, thirds,
+           mine, turned, total, near, far, corr, hid_one, hid_two, held_one, held_two, wide_one, wide_two, thirds,
            send_sem, recv_sem, local_sem):
     rows, cols, chans = feat.shape[1:]
     hid = b_one.shape[1]
@@ -223,42 +227,76 @@
         jnp.where(sec < secs - 1, offsets[sec], 0),
     )
 
+    spans = rows + 10
+
     def turn():
+        turned[0:4] = jnp.zeros((4, cols, chans), turned.dtype)
+        turned[rows + 10:] = jnp.zeros((4, cols, chans), turned.dtype)
+
         def one(r, carry):
-            mine[r] = jnp.dot(flip, mine[r], preferred_element_type=jnp.float32).astype(mine.dtype)
+            turned[r + 4] = jnp.dot(flip, mine[r], preferred_element_type=jnp.float32).astype(mine.dtype)
             return carry
 
         lax.fori_loop(0, rows + 6, one, 0)
 
-    group = 6 if rows % 6 == 0 else 2
+        def clear(r, carry):
+            for slot in range(2):
+                total[slot, r] = jnp.zeros((cols, cols), jnp.float32)
+            return carry
+
+        lax.fori_loop(0, spans, clear, 0)
+
+    def shift_of(slot):
+        return jnp.where(slot == 0, shifts[0], shifts[1])
+
+    def block(wide, slot, at, wides, start, number):
+        here = turned[pl.ds(start + 2 - shift_of(slot), number)].reshape(number * cols, chans)
+        there = wide[pl.ds(at, wides)].reshape(wides * cols, chans)
+        tile = lax.dot_general(here, there, (((1,), (1,)), ((), ())), preferred_element_type=jnp.float32)
+        for i in range(number):
+            found = total[slot, start + i]
+            for u in range(wides):
+                a = at + u - start - i
+                if 0 <= a < TAPS:
+                    band = skewed(tile[i * cols:(i + 1) * cols, u * cols:(u + 1) * cols], a * TAPS + 5)
+                    found = jnp.where((lane >= a * TAPS) & (lane < a * TAPS + TAPS), band, found)
+            total[slot, start + i] = found
+
+    def own(wide, slot, begin, end):
+        def step(k, carry):
+            at = SIDE + 2 * k
+            here = turned[pl.ds(at - 6 - shift_of(slot), 10)].reshape(10 * cols, chans)
+            there = wide[pl.ds(at, 2)].reshape(2 * cols, chans)
+            tile = lax.dot_general(here, there, (((1,), (1,)), ((), ())), preferred_element_type=jnp.float32)
+            for i in range(10):
+                found = total[slot, at - 8 + i]
+                for u in range(2):
+                    a = 8 + u - i
+                    if 0 <= a < TAPS:
+                        band = skewed(tile[i * cols:(i + 1) * cols, u * cols:(u + 1) * cols], a * TAPS + 5)
+                        found = jnp.where((lane >= a * TAPS) & (lane < a * TAPS + TAPS), band, found)
+                total[slot, at - 8 + i] = found
+            return carry
+
+        lax.fori_loop(begin, end, step, 0)
 
     def relate(wide, slot):
-        shift = jnp.where(slot == 0, shifts[0], shifts[1])
-
-        def step(g, carry):
-            base = g * group
-            here = mine[pl.ds(base, group)].reshape(group * cols, chans)
-            products = {}
-            for t in range(0, group + TAPS - 1, 2):
-                low, high = max(0, t - TAPS + 1), min(group, t + 2)
-                there = wide[pl.ds(base + 2 + shift + t, 2)].reshape(2 * cols, chans)
-                tile = lax.dot_general(
-                    here[low * cols:high * cols], there, (((1,), (1,)), ((), ())), preferred_element_type=jnp.float32
-                )
-                for i in range(low, high):
-                    for u in range(2):
-                        if 0 <= t + u - i < TAPS:
-                            products[i, t + u - i] = tile[(i - low) * cols:(i - low + 1) * cols, u * cols:(u + 1) * cols]
-            for i in range(group):
-                found = skewed(products[i, 0], 5)
-                for a in range(1, TAPS):
-                    found = jnp.where(lane >= a * TAPS, skewed(products[i, a], a * TAPS + 5), found)
-                corr[slot, base + i] = (found * gain).astype(corr.dtype)
+        block(wide, slot, 0, 1, 0, 1)
+        for at in range(1, SIDE, 2):
+            start = max(0, at - 8)
+            block(wide, slot, at, 2, start, at + 2 - start)
+        for at in range(SIDE + rows, 2 * SIDE + rows - 1, 2):
+            block(wide, slot, at, 2, at - 8, min(spans, at + 2) - at + 8)
+        at = 2 * SIDE + rows - 1
+        block(wide, slot, at, 1, at - 8, spans - at + 8)
+
+        def finish(r, carry):
+            corr[slot, r] = jnp.where(gain > 0, total[slot, r + 2 + shift_of(slot)] * scale, 0.0).astype(corr.dtype)
             return carry
 
-        lax.fori_loop(0, (rows + 6) // group, step, 0)
-
-    exchange(secs, strips, feat, mine, near, far, send_sem, recv_sem, loads, prepare, turn, relate)
+        lax.fori_loop(0, rows + 6, finish, 0)
+
+    exchange(secs, strips, feat, mine, near, far, send_sem, recv_sem, loads, prepare, turn, own, relate)
 
     convolve((corr.at[0], corr.at[1]), wide_one, b_one, hid_one)
 
@@ -291,13 +329,13 @@
         before = jnp.where(at_lane == 0, 0.0, pltpu.roll(total, 1, 1))
         after = jnp.where(at_lane == cols - 1, 0.0, pltpu.roll(total, cols - 1, 1))
         found.append(before[0:2] + total[2:4] + after[4:6])
-    turned = jnp.dot(
+    straight = jnp.dot(
         jnp.concatenate(found, axis=0), flip.astype(jnp.float32),
         preferred_element_type=jnp.float32, precision=lax.Precision.HIGHEST,
     )
     for r in range(rows):
         for p in range(2):
-            out[p * rows + r] = turned[2 * r + p:2 * r + p + 1]
+            out[p * rows + r] = straight[2 * r + p:2 * r + p + 1]
 
 
 def body(secs, strips, features, offsets, state, w_first, b_first, w_second, b_second, w_third):
@@ -313,6 +351,8 @@
         out_specs=VMEM,
         scratch_shapes=[
             pltpu.VMEM((rows + 6, cols, chans), bf16),
+            pltpu.VMEM((rows + 14, cols, chans), bf16),
+            pltpu.VMEM((2, rows + 10, cols, cols), jnp.float32),
             pltpu.VMEM((rows + 2 * SIDE, cols, chans), bf16),
             pltpu.VMEM((rows + 2 * SIDE, cols, chans), bf16),
             pltpu.VMEM((2, rows + 6, cols, cols), bf16),

time: 33.2 us -> 38 us (1.14)
  Pallas kernels: 31.6 us -> 36.4 us
    pallas_call x1, Pallas kernels: 31.6 us -> 36.4 us  [body(): pl.pallas_call(functools.partial(kernel, secs, strips), out_shape=jax.Sha...]
where the time goes in v4:
time: 38 us; the launch traced here: 37.8 us
  Pallas kernels  36.4 us (96%)
  other arithmetic  1.32 us (3%)
    pallas_call x1, Pallas kernels, body(): pl.pallas_call(functools.partial(kernel, secs, strips), out_shape=jax.Sha...  36.4 us
    add x1, other arithmetic, body(): return state + delta.reshape(state.shape)  1.32 us

profile of v4, /device:TPU:18, one launch (start us, length us, event | category | flops | bytes accessed | tf_op | source)
XLA Modules:
  0.0 37.8 jit_solution(6599460868796043976)
XLA Ops:
  0.0 0.0 copy-start
  0.0 36.4 %shard_map.82 = f32[24,1,128]{2,1,0:T(1,128)} custom-call(bf16[1,12,128,128]{3,2,1,0:T(8,128)(2,1)} %feat.1, s32[4]{0:T(128)} %offsets.1, bf16[3,3,162,128]{3,2,1,0:T(8,128)(2,1)} %w_one.1, f32[1,128]{1,0:T(1,128)} %bitcast.6, bf16[3,3,128,128]{3,2,1,0:T(8,128)(2,1)} %w_two.1, f32[1,128]{1,0:T(1,128)} %bitcast.7, bf16[3,3,2,128]{3,2,1,0:T(2,128)(2,1)} %bitcast.5), custom_call_target="tpu_custom_call" | custom-call | tf_op jit(solution)/shard_map/pallas_call | solution.py:347
  36.4 0.0 copy-done
  36.5 1.3 %add.3 = f32[2,1,12,128]{3,1,2,0:T(1,128)} add(f32[2,1,12,128]{3,1,2,0:T(1,128)S(1)} %copy-done, f32[2,1,12,128]{3,1,2,0:T(1,128)} %bitcast.4) | non-fusion elementwise | flops 3072 | bytes 36864 | tf_op jit(solution)/shard_map/add | solution.py:375
Async XLA Ops:
  0.0 36.5 %copy-start = (f32[2,1,12,128]{3,1,2,0:T(1,128)S(1)}, f32[2,1,12,128]{3,1,2,0:T(1,128)}, u32[]{:S(2)}) copy-start(f32[2,1,12,128]{3,1,2,0:T(1,128)} %param.10) | copy-start | bytes 36868
